TPU v7x, 32 devices: a whole 2x2x4 slice. The times are simulated.
32 devices in a mesh: face: 8 (over z, x), band: 4 (over y, core).
Axes of the slice: x: 2, y: 2, z: 4, core: 2. Of those that a mesh axis runs over, the one named last changes fastest.
Arguments:
- node_latents: bfloat16 [8192, 512], P(('face', 'band')), may hold values from -6 to 6
- coarse_latents: bfloat16 [1024, 512], replicated, may hold values from -6 to 6
- edge_latents: bfloat16 [32768, 512], P(('face', 'band')), may hold values from -6 to 6
- up_latents: bfloat16 [8192, 512], P(('face', 'band')), may hold values from -6 to 6
- edge_weight_in: bfloat16 [1536, 512], replicated, may hold values from -0.15625 to 0.15625
- edge_weight_out: bfloat16 [512, 512], replicated, may hold values from -0.25 to 0.25
- edge_gain: float32 [512], replicated, may hold values from 0.5 to 1.5
- node_weight_in: bfloat16 [1024, 512], replicated, may hold values from -0.1875 to 0.1875
- node_weight_out: bfloat16 [512, 512], replicated, may hold values from -0.25 to 0.25
- node_gain: float32 [512], replicated, may hold values from 0.5 to 1.5
- nodes_cotangent: bfloat16 [8192, 512], P(('face', 'band')), may hold values from -6 to 6
- coarse_cotangent: bfloat16 [1024, 512], replicated, may hold values from -6 to 6
- edges_cotangent: bfloat16 [32768, 512], P(('face', 'band')), may hold values from -6 to 6
- ups_cotangent: bfloat16 [8192, 512], P(('face', 'band')), may hold values from -6 to 6
- send_rows: int32 [32, 32, 4], P(('face', 'band')), may hold values from 0 to 255, as said below
- edge_sender: int32 [32768], P(('face', 'band')), may hold values from 0 to 1407, as said below
- edge_receiver: int32 [32768], P(('face', 'band')), may hold values from 0 to 255
- up_sender: int32 [8192], P(('face', 'band')), may hold values from 0 to 255
- up_receiver: int32 [8192], P(('face', 'band')), may hold values from 0 to 1023
Outputs:
- grad_nodes: float32 [8192, 512], P(('face', 'band'))
- grad_coarse: float32 [1024, 512], replicated
- grad_edges: float32 [32768, 512], P(('face', 'band'))
- grad_ups: float32 [8192, 512], P(('face', 'band'))
- grad_edge_in: float32 [1536, 512], replicated
- grad_edge_out: float32 [512, 512], replicated
- grad_edge_gain: float32 [512], replicated
- grad_node_in: float32 [1024, 512], replicated
- grad_node_out: float32 [512, 512], replicated
- grad_node_gain: float32 [512], replicated
Inputs may be any that keep to these rules, and one draw needn't show every extreme that they name: `send_rows`: entry [s, p, k] is a row of device s's nodes sent to device p in slot k. Each pair uses its first few slots, at most 4; every device fills all 4 slots to at least one device, and in every draw some device receives 4 rows from every device. Unused slots hold 0 and no edge reads them. `edge_sender`: an edge of device p reads row t of p's sender table: its own node t below 256; slot k of the rows that device s sends to p for t = 256 + s * 4 + k, always a used slot; coarse node t - 384 from 384 on.
All inputs are finite; a program needn't handle non-finite values.
Results may differ from a plain program's by a relative error of at most 0.0068.
Values may be sent and summed in bfloat16 or wider, within the bound.
No kernel may reach another device: no remote copies, remote signals or barrier semaphores. Data moves between devices by JAX's collectives and lax.ppermute only.
A program may use at most 192 MiB of HBM per device.

v0:
```python
import math
import jax
import jax.numpy as jnp
from jax import lax
from jax.sharding import PartitionSpec as P

EPSILON = 1e-05


def mlp_forward(inputs, residual_base, first_weight, second_weight, gain_vec):
    pre_act = jnp.dot(inputs, first_weight, preferred_element_type=jnp.float32)
    hidden_act = jax.nn.silu(pre_act).astype(jnp.bfloat16)
    projected = jnp.dot(hidden_act, second_weight, preferred_element_type=jnp.float32)
    center = projected - jnp.mean(projected, axis=1, keepdims=True)
    inv_std = lax.rsqrt(jnp.mean(center * center, axis=1, keepdims=True) + EPSILON)
    normed = center * inv_std
    return (residual_base + normed * gain_vec, (pre_act, hidden_act, normed, inv_std))


def mlp_backward(inputs, first_weight, second_weight, gain_vec, cache_vals, cotangent):
    pre_act, hidden_act, normed, inv_std = cache_vals
    grad_gain = jnp.sum(cotangent * normed, axis=0)
    scaled = cotangent * gain_vec
    grad_proj = inv_std * (
        scaled
        - jnp.mean(scaled, axis=1, keepdims=True)
        - normed * jnp.mean(scaled * normed, axis=1, keepdims=True)
    )
    grad_proj = grad_proj.astype(jnp.bfloat16)
    grad_second = jnp.dot(hidden_act.T, grad_proj, preferred_element_type=jnp.float32)
    grad_hidden = jnp.dot(grad_proj, second_weight.T, preferred_element_type=jnp.float32)
    logistic = jax.nn.sigmoid(pre_act)
    grad_pre = (grad_hidden * logistic * (1.0 + pre_act * (1.0 - logistic))).astype(jnp.bfloat16)
    grad_first = jnp.dot(inputs.T, grad_pre, preferred_element_type=jnp.float32)
    grad_inputs = jnp.dot(grad_pre, first_weight.T, preferred_element_type=jnp.float32)
    return (grad_inputs, grad_first, grad_second, grad_gain)


def per_device(
    node_latents,
    coarse_latents,
    edge_latents,
    up_latents,
    edge_weight_in,
    edge_weight_out,
    edge_gain,
    node_weight_in,
    node_weight_out,
    node_gain,
    nodes_cotangent,
    coarse_cotangent,
    edges_cotangent,
    ups_cotangent,
    send_rows,
    edge_sender,
    edge_receiver,
    up_sender,
    up_receiver,
):
    latent_width = node_latents.shape[1]
    node_count = node_latents.shape[0]
    coarse_count = coarse_latents.shape[0]
    devices = lax.axis_size(("face", "band"))
    slot_count = send_rows.shape[2]
    import_count = devices * slot_count
    send_table = send_rows[0]
    outgoing = jnp.take(node_latents, send_table, axis=0)
    face_count = lax.axis_size("face")
    sectioned = outgoing.reshape(face_count, devices // face_count, slot_count, latent_width)
    incoming = lax.all_to_all(
        lax.all_to_all(sectioned, "face", split_axis=0, concat_axis=0, tiled=True),
        "band",
        split_axis=1,
        concat_axis=1,
        tiled=True,
    )
    sender_table = jnp.concatenate(
        [node_latents, incoming.reshape(import_count, latent_width), coarse_latents], 0
    )
    edge_inputs = jnp.concatenate(
        [
            edge_latents,
            jnp.take(sender_table, edge_sender, axis=0),
            jnp.take(node_latents, edge_receiver, axis=0),
        ],
        1,
    )
    edge_output, edge_cache = mlp_forward(
        edge_inputs, edge_latents.astype(jnp.float32), edge_weight_in, edge_weight_out, edge_gain
    )
    new_edges = edge_output.astype(jnp.bfloat16)
    receiver_onehot = (
        jnp.arange(node_count, dtype=jnp.int32)[:, None] == edge_receiver[None, :]
    ).astype(jnp.bfloat16)
    fine_total = jnp.dot(receiver_onehot, new_edges, preferred_element_type=jnp.float32)
    up_inputs = jnp.concatenate(
        [
            up_latents,
            jnp.take(node_latents, up_sender, axis=0),
            jnp.take(coarse_latents, up_receiver, axis=0),
        ],
        1,
    )
    up_output, up_cache = mlp_forward(
        up_inputs, up_latents.astype(jnp.float32), edge_weight_in, edge_weight_out, edge_gain
    )
    new_ups = up_output.astype(jnp.bfloat16)
    node_inputs = jnp.concatenate([node_latents, fine_total.astype(jnp.bfloat16)], 1)
    unused_node, node_cache = mlp_forward(
        node_inputs, node_latents.astype(jnp.float32), node_weight_in, node_weight_out, node_gain
    )
    node_grad_inputs, node_first, node_second, node_gain_grad = mlp_backward(
        node_inputs,
        node_weight_in,
        node_weight_out,
        node_gain,
        node_cache,
        nodes_cotangent.astype(jnp.float32),
    )
    row_ids = jnp.arange(coarse_count, dtype=jnp.int32)
    onehot_rows = (row_ids[:, None] == up_receiver[None, :]).astype(jnp.bfloat16)
    coarse_total = lax.psum(
        jnp.dot(onehot_rows, new_ups, preferred_element_type=jnp.float32), ("face", "band")
    )
    coarse_inputs = jnp.concatenate([coarse_latents, coarse_total.astype(jnp.bfloat16)], 1)
    unused_coarse, coarse_cache = mlp_forward(
        coarse_inputs,
        coarse_latents.astype(jnp.float32),
        node_weight_in,
        node_weight_out,
        node_gain,
    )
    coarse_grad_inputs, coarse_first, coarse_second, coarse_gain_grad = mlp_backward(
        coarse_inputs,
        node_weight_in,
        node_weight_out,
        node_gain,
        coarse_cache,
        coarse_cotangent.astype(jnp.float32),
    )
    coarse_grad = coarse_grad_inputs[:, latent_width:]
    coarse_after = coarse_cotangent.astype(jnp.float32) + coarse_grad_inputs[:, :latent_width]
    node_first_total, node_second_total, node_gain_total = (node_first, node_second, node_gain_grad)
    extra_first, extra_second, extra_gain = (coarse_first, coarse_second, coarse_gain_grad)
    up_cotangent = ups_cotangent.astype(jnp.float32) + jnp.take(coarse_grad, up_receiver, axis=0)
    up_grad_inputs, up_first, up_second, up_gain_grad = mlp_backward(
        up_inputs, edge_weight_in, edge_weight_out, edge_gain, up_cache, up_cotangent
    )
    grad_ups = up_cotangent + up_grad_inputs[:, :latent_width]
    fine_grad = node_grad_inputs[:, latent_width:]
    edge_cotangent = edges_cotangent.astype(jnp.float32) + jnp.take(
        fine_grad, edge_receiver, axis=0
    )
    edge_grad_inputs, edge_first, edge_second, edge_gain_grad = mlp_backward(
        edge_inputs, edge_weight_in, edge_weight_out, edge_gain, edge_cache, edge_cotangent
    )
    grad_edges = edge_cotangent + edge_grad_inputs[:, :latent_width]
    table_grad = jax.ops.segment_sum(
        edge_grad_inputs[:, latent_width : 2 * latent_width],
        edge_sender,
        num_segments=node_count + import_count + coarse_count,
    )
    returning = table_grad[node_count : node_count + import_count].reshape(
        devices, slot_count, latent_width
    )
    face_count = lax.axis_size("face")
    sectioned_back = returning.reshape(face_count, devices // face_count, slot_count, latent_width)
    returned = lax.all_to_all(
        lax.all_to_all(
            sectioned_back.astype(jnp.bfloat16), "face", split_axis=0, concat_axis=0, tiled=True
        ),
        "band",
        split_axis=1,
        concat_axis=1,
        tiled=True,
    ).astype(sectioned_back.dtype)
    grad_nodes = (
        nodes_cotangent.astype(jnp.float32)
        + node_grad_inputs[:, :latent_width]
        + table_grad[:node_count]
        + jax.ops.segment_sum(
            edge_grad_inputs[:, 2 * latent_width :], edge_receiver, num_segments=node_count
        )
        + jax.ops.segment_sum(
            up_grad_inputs[:, latent_width : 2 * latent_width], up_sender, num_segments=node_count
        )
        + jax.ops.segment_sum(
            returned.reshape(import_count, latent_width),
            send_table.reshape(import_count),
            num_segments=node_count,
        )
    )
    coarse_local = table_grad[node_count + import_count :] + jax.ops.segment_sum(
        up_grad_inputs[:, 2 * latent_width :], up_receiver, num_segments=coarse_count
    )
    edge_first_total = edge_first + up_first
    edge_second_total = edge_second + up_second
    edge_gain_total = edge_gain_grad + up_gain_grad
    summed = lax.psum(
        (
            node_first_total,
            node_second_total,
            node_gain_total,
            coarse_local,
            edge_first_total,
            edge_second_total,
            edge_gain_total,
        ),
        ("face", "band"),
    )
    node_summed = (summed[0], summed[1], summed[2])
    edge_summed = (summed[3], summed[4], summed[5], summed[6])
    edge_rows_total = (edge_latents.shape[0] + up_latents.shape[0]) * devices
    node_rows_total = node_count * devices + coarse_count
    edge_scale = 1.0 / math.sqrt(edge_rows_total)
    node_scale = 1.0 / math.sqrt(node_rows_total)
    grad_coarse = edge_summed[0] + coarse_after
    return (
        grad_nodes,
        grad_coarse,
        grad_edges,
        grad_ups,
        edge_summed[1] * edge_scale,
        edge_summed[2] * edge_scale,
        edge_summed[3] * edge_scale,
        (node_summed[0] + extra_first) * node_scale,
        (node_summed[1] + extra_second) * node_scale,
        (node_summed[2] + extra_gain) * node_scale,
    )


def solution(mesh):
    return jax.shard_map(
        per_device,
        mesh=mesh,
        in_specs=(
            P(("face", "band"), None),
            P(),
            P(("face", "band"), None),
            P(("face", "band"), None),
            P(),
            P(),
            P(),
            P(),
            P(),
            P(),
            P(("face", "band"), None),
            P(),
            P(("face", "band"), None),
            P(("face", "band"), None),
            P(("face", "band"), None, None),
            P(("face", "band")),
            P(("face", "band")),
            P(("face", "band")),
            P(("face", "band")),
        ),
        out_specs=(
            P(("face", "band"), None),
            P(),
            P(("face", "band"), None),
            P(("face", "band"), None),
            P(),
            P(),
            P(),
            P(),
            P(),
            P(),
        ),
        check_vma=False,
    )
```

profile of v0, /device:TPU:0, one launch (start us, length us, event | category | flops | bytes accessed | tf_op | source)
XLA Modules:
  0.0 416.2 jit_solution(11921928592498029254)
XLA Ops:
  9.2 1.9 gather_fusion
  11.9 7.3 %all-to-all-start = ((bf16[8,4,4,512]{3,2,1,0:T(4,128)(2,1)}), bf16[8,4,4,512]{3,2,1,0:T(4,128)(2,1)}, u32[]{:S(2)}, u32[]{:S(2)}) async-start(bf16[8,4,4,512]{3,2,1,0:T(4,128)(2,1)} %broadcast_select_fusion.4), calls=%async_computation | async-start | bytes 262144 | tf_op jit(solution)/shard_map/all_to_all | solution.py:71
  24.5 1.6 fusion.40
  27.3 1.9 fusion.22
  29.2 61.8 %all-reduce.6 = bf16[1024,512]{1,0:T(8,128)(2,1)} all-reduce(f32[1024,512]{1,0:T(8,128)} %fusion.22), channel_id=1, replica_groups=mesh['face'=8,'band'=4] {'face','band'}, use_global_device_ids=true, to_apply=%region_12.13 | all-reduce | flops 524288 | bytes 3145728 | tf_op jit(solution)/shard_map/psum | solution.py:122
  91.0 2.8 fusion.15
  93.9 2.2 fusion.66
  96.0 3.0 copy.111
  99.0 2.1 multiply_reduce_fusion.1
  101.2 1.6 fusion.8
  107.2 2.0 copy-done.13
  109.3 1.5 slice.72
  110.8 2.8 gather_fusion.6
  116.7 1.8 fusion.70
  119.0 1.6 copy.104
  120.6 3.3 all-to-all-start.1
  126.5 4.0 gather_fusion.2
  131.7 2.3 copy.109
  136.1 5.1 %gather_fusion.1 = bf16[1024,512]{1,0:T(8,128)(2,1)} fusion(bf16[1408,512]{1,0:T(8,128)(2,1)S(1)} %pad_maximum_fusion.2, s32[1024]{0:T(1024)S(1)} %fusion.45), kind=kCustom, calls=%fused_computation.1 | custom fusion | bytes 2101248 | tf_op jit(solution)/shard_map/jit(_take)/gather | solution.py:83
  141.2 2.4 copy.106
  145.1 1.8 fusion.17
  155.0 1.8 fusion.38
  156.8 4.9 %gather_fusion.3 = f32[1024,512]{1,0:T(8,128)} fusion(f32[256,512]{1,0:T(8,128)S(1)} %slice.68, s32[1024]{0:T(1024)S(1)} %fusion.46), kind=kCustom, calls=%fused_computation.3 | custom fusion | bytes 4198400 | tf_op jit(solution)/shard_map/jit(_take)/gather | solution.py:151
  161.6 3.1 copy.110
  164.8 3.3 multiply_reduce_fusion
  172.5 1.8 fusion.16
  174.3 4.5 %fusion.68 = f32[1024,1536]{1,0:T(8,128)} fusion(bf16[1024,512]{1,0:T(8,128)(2,1)S(1)} %multiply_convert_fusion.2, bf16[1536,512]{1,0:T(8,128)(2,1)S(1)} %copy-done), kind=kOutput, calls=%fused_computation.170 | convolution fusion | flops 1610612736 | bytes 8912896 | tf_op jit(solution)/shard_map/dot_general | solution.py:35
  178.8 2.3 convolution_add_fusion
  181.1 1.7 convolution_add_fusion.2
  182.9 9.1 %scatter_custom_fusion = f32[1408,512]{1,0:T(8,128)} fusion(s32[1024]{0:T(1024)} %param.34, f32[1024,1536]{1,0:T(8,128)} %fusion.68, f32[]{:T(128)} %constant.129.clone.1), kind=kCustom, calls=%fused_computation.28 | custom fusion | flops 524288 | bytes 4981248 | tf_op jit(solution)/shard_map/scatter-add | solution.py:158
  192.0 3.2 slice.75
  195.2 5.1 %scatter_custom_fusion.4 = f32[1024,512]{1,0:T(8,128)} fusion(f32[1024,512]{1,0:T(8,128)} %slice.75, s32[256]{0:T(256)} %param.37, f32[256,1536]{1,0:T(8,128)S(1)} %copy-done.11), kind=kCustom, calls=%fused_computation.83 | custom fusion | flops 131072 | bytes 2621440 | tf_op jit(solution)/shard_map/scatter-add | solution.py:193
  201.1 3.2 scatter_custom_fusion.2
  204.4 1.9 slice_add_fusion
  208.1 4.6 %all-to-all-start.2 = ((bf16[8,4,4,512]{3,2,1,0:T(4,128)(2,1)}), bf16[8,4,4,512]{3,2,1,0:T(4,128)(2,1)S(1)}, u32[]{:S(2)}, u32[]{:S(2)}) async-start(bf16[8,4,4,512]{3,2,1,0:T(4,128)(2,1)} %convert_element_type.97), calls=%async_computation.2 | async-start | bytes 262144 | tf_op jit(solution)/shard_map/all_to_all | solution.py:169
  214.1 42.8 %all-reduce = (f32[512]{0:T(512)S(1)}, f32[512]{0:T(512)S(1)}) all-reduce(f32[512]{0:T(512)S(1)} %add.244, f32[512]{0:T(512)S(1)} %copy-done.51), channel_id=1, replica_groups=mesh['face'=8,'band'=4] {'face','band'}, use_global_device_ids=true, to_apply=%region_27.28 | all-reduce | flops 1024 | bytes 8192 | tf_op jit(solution)/shard_map/psum | solution.py:199
  258.2 3.5 all-to-all-start.3
  262.3 3.3 slice.78
  265.6 2.9 copy.118
  268.5 4.1 add.240
  272.6 2.9 copy.117
  275.5 7.6 %scatter_custom_fusion.1 = f32[256,512]{1,0:T(8,128)S(1)} fusion(f32[256,512]{1,0:T(8,128)S(1)} %fusion.30, s32[1024]{0:T(1024)S(1)} %copy-done.48, f32[1024,1536]{1,0:T(8,128)} %fusion.68), kind=kCustom, calls=%fused_computation.26 | custom fusion | flops 524288 | bytes 2621440 | tf_op jit(solution)/shard_map/scatter-add | solution.py:181
  283.6 1.6 scatter_fusion
  285.1 111.2 %all-reduce.5.cloned.1.call-done = (f32[1024,512]{1,0:T(8,128)}, f32[1536,512]{1,0:T(8,128)}, f32[512,512]{1,0:T(8,128)}, f32[1024,512]{1,0:T(8,128)}, f32[512,512]{1,0:T(8,128)}) async-done(((f32[1024,512]{1,0:T(8,128)}, f32[1536,512]{1,0:T(8,128)}, f32[512,512]{1,0:T(8,128)}, f32[1024,512]{1,0:T(8,128)}, f32[512,512]{1,0:T(8,128)}), (f32[1024,512]{1,0:T(8,128)}, f32[1536,512]{1,0:T(8,128)}, ...) | async-done | bytes 9437200 | tf_op jit(solution)/shard_map/psum | solution.py:199
  396.3 3.8 fusion.14
  400.1 2.6 add_multiply_fusion
  404.1 1.9 fusion.7
  407.0 2.0 broadcast_multiply_fusion
  (229 shorter events, 45.5 us)
Async XLA Ops:
  7.2 17.3 %copy-start = (bf16[1536,512]{1,0:T(8,128)(2,1)S(1)}, bf16[1536,512]{1,0:T(8,128)(2,1)}, u32[]{:S(2)}) copy-start(bf16[1536,512]{1,0:T(8,128)(2,1)} %param.23) | copy-start | bytes 4718596
  7.2 14.7 %copy-start.1 = (bf16[256,512]{1,0:T(8,128)(2,1)S(1)}, bf16[256,512]{1,0:T(8,128)(2,1)}, u32[]{:S(2)}) copy-start(bf16[256,512]{1,0:T(8,128)(2,1)} %param.19) | copy-start | bytes 786436
  11.0 12.1 %copy-start.9 = (bf16[1024,512]{1,0:T(8,128)(2,1)S(1)}, bf16[1024,512]{1,0:T(8,128)(2,1)}, u32[]{:S(2)}) copy-start(bf16[1024,512]{1,0:T(8,128)(2,1)} %param.20) | copy-start | bytes 3145732
  11.9 107.2 %all-to-all-start = ((bf16[8,4,4,512]{3,2,1,0:T(4,128)(2,1)}), bf16[8,4,4,512]{3,2,1,0:T(4,128)(2,1)}, u32[]{:S(2)}, u32[]{:S(2)}) async-start(bf16[8,4,4,512]{3,2,1,0:T(4,128)(2,1)} %broadcast_select_fusion.4), calls=%async_computation | async-start | bytes 262144 | tf_op jit(solution)/shard_map/all_to_all | solution.py:71
  24.5 2.1 copy-start.26
  91.0 2.8 copy-start.56
  93.8 2.2 copy-start.68
  96.0 5.1 %copy-start.7 = (bf16[1024,512]{1,0:T(8,128)(2,1)S(1)}, bf16[1024,512]{1,0:T(8,128)(2,1)}, u32[]{:S(2)}) copy-start(bf16[1024,512]{1,0:T(8,128)(2,1)} %param.30) | copy-start | bytes 3145732
  99.0 2.2 copy-start.2
  99.0 2.2 copy-start.44
  102.8 1.9 copy-start.69
  107.2 2.0 copy-start.13
  110.8 2.9 copy-start.42
  116.7 2.3 copy-start.46
  116.7 8.4 %copy-start.28 = (bf16[1024,512]{1,0:T(8,128)(2,1)S(1)}, bf16[1024,512]{1,0:T(8,128)(2,1)}, u32[]{:S(2)}) copy-start(bf16[1024,512]{1,0:T(8,128)(2,1)} %param.21) | copy-start | bytes 3145732
  120.6 13.4 %all-to-all-start.1 = ((bf16[8,4,4,512]{3,2,0,1:T(4,128)(2,1)}), bf16[8,4,4,512]{3,2,0,1:T(4,128)(2,1)S(1)}, u32[]{:S(2)}, u32[]{:S(2)}) async-start(bf16[8,4,4,512]{3,2,0,1:T(4,128)(2,1)} %copy.104), calls=%async_computation.1 | async-start | bytes 262144 | tf_op jit(solution)/shard_map/all_to_all | solution.py:70
  124.0 272.3 %all-reduce.5.cloned.1.call-start = ((), (), s32[]{:S(2)}) async-start(), calls=%async_computation.4 | async-start | bytes 18874368 | tf_op jit(solution)/shard_map/psum | solution.py:199
  141.2 2.4 copy-start.17
  141.2 2.4 copy-start.49
  141.2 2.4 copy-start.54
  145.0 1.9 copy-start.36
  145.1 1.9 copy-start.38
  161.6 3.1 copy-start.15
  164.8 3.4 copy-start.5
  168.2 2.5 copy-start.71
  174.3 4.5 %copy-start.25 = (bf16[256,512]{1,0:T(8,128)(2,1)S(1)}, bf16[256,512]{1,0:T(8,128)(2,1)}, u32[]{:S(2)}) copy-start(bf16[256,512]{1,0:T(8,128)(2,1)} %copy-done.24) | copy-start | bytes 786436
  174.3 4.5 %copy-start.27 = (bf16[256,512]{1,0:T(8,128)(2,1)S(1)}, bf16[256,512]{1,0:T(8,128)(2,1)}, u32[]{:S(2)}) copy-start(bf16[256,512]{1,0:T(8,128)(2,1)} %copy-done.26) | copy-start | bytes 786436
  174.3 4.5 %copy-start.41 = (bf16[256,512]{1,0:T(8,128)(2,1)S(1)}, bf16[256,512]{1,0:T(8,128)(2,1)}, u32[]{:S(2)}) copy-start(bf16[256,512]{1,0:T(8,128)(2,1)} %param.22) | copy-start | bytes 786436
  178.8 2.3 copy-start.65
  192.0 3.2 copy-start.11
  201.0 11.7 %copy-start.23 = (bf16[256,512]{1,0:T(8,128)(2,1)S(1)}, bf16[256,512]{1,0:T(8,128)(2,1)}, u32[]{:S(2)}) copy-start(bf16[256,512]{1,0:T(8,128)(2,1)} %param.29) | copy-start | bytes 786436
  204.4 9.7 %copy-start.52 = (f32[512]{0:T(512)S(1)}, f32[512]{0:T(512)}, u32[]{:S(2)}) copy-start(f32[512]{0:T(512)} %get-tuple-element.76) | copy-start | bytes 6148
  204.4 9.7 %copy-start.51 = (f32[512]{0:T(512)S(1)}, f32[512]{0:T(512)}, u32[]{:S(2)}) copy-start(f32[512]{0:T(512)} %get-tuple-element.78) | copy-start | bytes 6148
  204.4 52.5 %copy-start.50 = (f32[512]{0:T(512)S(1)}, f32[512]{0:T(512)}, u32[]{:S(2)}) copy-start(f32[512]{0:T(512)} %get-tuple-element.72) | copy-start | bytes 6148
  208.1 49.4 %all-to-all-start.2 = ((bf16[8,4,4,512]{3,2,1,0:T(4,128)(2,1)}), bf16[8,4,4,512]{3,2,1,0:T(4,128)(2,1)S(1)}, u32[]{:S(2)}, u32[]{:S(2)}) async-start(bf16[8,4,4,512]{3,2,1,0:T(4,128)(2,1)} %convert_element_type.97), calls=%async_computation.2 | async-start | bytes 262144 | tf_op jit(solution)/shard_map/all_to_all | solution.py:169
  258.2 25.1 %all-to-all-start.3 = ((bf16[8,4,4,512]{3,2,0,1:T(4,128)(2,1)}), bf16[8,4,4,512]{3,2,0,1:T(4,128)(2,1)S(1)}, u32[]{:S(2)}, u32[]{:S(2)}) async-start(bf16[8,4,4,512]{3,2,0,1:T(4,128)(2,1)} %copy.113), calls=%async_computation.3 | async-start | bytes 262144 | tf_op jit(solution)/shard_map/all_to_all | solution.py:168
  275.5 7.7 %copy-start.20 = (f32[256,512]{1,0:T(8,128)S(1)}, f32[256,512]{1,0:T(8,128)}, u32[]{:S(2)}) copy-start(f32[256,512]{1,0:T(8,128)} %scatter_custom_fusion.2) | copy-start | bytes 1572868
  283.6 112.7 %copy-start.35 = (bf16[1024,512]{1,0:T(8,128)(2,1)S(1)}, bf16[1024,512]{1,0:T(8,128)(2,1)}, u32[]{:S(2)}) copy-start(bf16[1024,512]{1,0:T(8,128)(2,1)} %copy-done.34) | copy-start | bytes 3145732
  285.1 115.0 %copy-start.6 = (f32[256,512]{1,0:T(8,128)}, f32[256,512]{1,0:T(8,128)S(1)}, u32[]{:S(2)}) copy-start(f32[256,512]{1,0:T(8,128)S(1)} %scatter_fusion) | copy-start | bytes 1572868
  396.3 3.8 copy-start.10
  396.3 3.8 copy-start.21
  396.3 3.8 copy-start.55
  396.3 3.8 copy-start.64
  400.1 2.6 copy-start.8
  400.1 3.1 copy-start.14
  400.1 3.9 copy-start.19
  404.1 1.9 copy-start.31
  404.1 3.0 copy-start.18
  (29 other events, 38.1 us)
Sparse Core Ops, SparseCore 0:
  200.4 195.8 all-reduce.4
where the time goes:
time: 421 us; the launch traced here: 416 us
  waiting for transfers between devices  111 us (26%)
  blocking collectives  105 us (25%)
  local copies, waits for them, and re-layouts  64.5 us (15%)
  other arithmetic  60 us (14%)
  matrix products  41.4 us (10%)
  starting transfers between devices  19.3 us (5%)
  between operations  15.2 us (4%)
    psum x1, waiting for transfers between devices, per_device(): lax.psum((node_first_total, node_second_total, node_gain_total, coarse_lo...  111 us
    psum x1, blocking collectives, per_device(): lax.psum(jnp.dot(onehot_rows, new_ups, preferred_element_type=jnp.float32...  61.8 us
    psum x1, blocking collectives, per_device(): lax.psum((node_first_total, node_second_total, node_gain_total, coarse_lo...  42.8 us
    unnamed x149, local copies, waits for them, and re-layouts  19.4 us
    scatter-add x1, other arithmetic, per_device(): jax.ops.segment_sum(edge_grad_inputs[:, latent_width:2 * latent_width], e...  9.1 us
    dot_general x4, matrix products, mlp_backward(): grad_first = jnp.dot(inputs.T, grad_pre, preferred_element_type=jnp.float32)  8.44 us
  transfers between devices with their start and end apart: 5, of which 1 were waited for; matrix products, arithmetic and copies ran while one was open for 18% of the time, Pallas kernels for 0%

commit v1 on v0

--- a/solution.py
+++ b/solution.py
@@ -57,6 +57,10 @@
     up_sender,
     up_receiver,
 ):
+
+    def refer_the_domain(inner_x):
+        return jnp.sum(jax.lax.all_gather(inner_x, ("face", "band")), axis=0)
+
     latent_width = node_latents.shape[1]
     node_count = node_latents.shape[0]
     coarse_count = coarse_latents.shape[0]
@@ -119,8 +123,8 @@
     )
     row_ids = jnp.arange(coarse_count, dtype=jnp.int32)
     onehot_rows = (row_ids[:, None] == up_receiver[None, :]).astype(jnp.bfloat16)
-    coarse_total = lax.psum(
-        jnp.dot(onehot_rows, new_ups, preferred_element_type=jnp.float32), ("face", "band")
+    coarse_total = refer_the_domain(
+        jnp.dot(onehot_rows, new_ups, preferred_element_type=jnp.float32)
     )
     coarse_inputs = jnp.concatenate([coarse_latents, coarse_total.astype(jnp.bfloat16)], 1)
     unused_coarse, coarse_cache = mlp_forward(

time: 421 us -> 658 us (1.56)
  waiting for transfers between devices: 111 us -> 384 us
  blocking collectives: 105 us -> 39.7 us
  other arithmetic: 60 us -> 82.9 us
    all_gather x0 -> x1, waiting for transfers between devices: none -> 268 us  [refer_the_domain(): return jnp.sum(jax.lax.all_gather(inner_x, ('face', 'band')), axis=0)]
    psum x1 -> x0, blocking collectives: 61.8 us -> none  [per_device(): lax.psum(jnp.dot(onehot_rows, new_ups, preferred_element_type=jnp.float32...]
    reduce_sum x0 -> x1, other arithmetic: none -> 22.1 us  [refer_the_domain(): return jnp.sum(jax.lax.all_gather(inner_x, ('face', 'band')), axis=0)]
    psum x1, waiting for transfers between devices: 111 us -> 99.4 us  [per_device(): lax.psum((node_first_total, node_second_total, node_gain_total, coarse_lo...]
    all_to_all x1, waiting for transfers between devices: 0.01 us -> 9.21 us  [per_device(): lax.all_to_all(sectioned_back.astype(jnp.bfloat16), 'face', split_axis=0,...]
    all_to_all x1, waiting for transfers between devices: 0.01 us -> 7.39 us  [per_device(): lax.all_to_all(sectioned, 'face', split_axis=0, concat_axis=0, tiled=True)]
    unnamed x149 -> x157, local copies, waits for them, and re-layouts: 19.4 us -> 24.2 us
  transfers between devices with their start and end apart: 5 -> 6, of which waited for: 1 -> 4; matrix products, arithmetic and copies ran while one was open for 18% -> 16% of each run, Pallas kernels for 0% -> 0%
where the time goes in v1:
time: 658 us; the launch traced here: 653 us
  waiting for transfers between devices  384 us (58%)
  other arithmetic  82.9 us (13%)
  local copies, waits for them, and re-layouts  70.5 us (11%)
  matrix products  42.6 us (6%)
  blocking collectives  39.7 us (6%)
  starting transfers between devices  18 us (3%)
  between operations  15.2 us (2%)
    all_gather x1, waiting for transfers between devices, refer_the_domain(): return jnp.sum(jax.lax.all_gather(inner_x, ('face', 'band')), axis=0)  268 us
    psum x1, waiting for transfers between devices, per_device(): lax.psum((node_first_total, node_second_total, node_gain_total, coarse_lo...  99.4 us
    psum x1, blocking collectives, per_device(): lax.psum((node_first_total, node_second_total, node_gain_total, coarse_lo...  39.7 us
    unnamed x157, local copies, waits for them, and re-layouts  24.2 us
    reduce_sum x1, other arithmetic, refer_the_domain(): return jnp.sum(jax.lax.all_gather(inner_x, ('face', 'band')), axis=0)  22.1 us
  transfers between devices with their start and end apart: 6, of which 4 were waited for; matrix products, arithmetic and copies ran while one was open for 16% of the time, Pallas kernels for 0%

profile of v1, /device:TPU:0, one launch (start us, length us, event | category | flops | bytes accessed | tf_op | source)
XLA Modules:
  0.0 652.5 jit_solution(7456087467410346280)
XLA Ops:
  10.1 2.6 gather_fusion.5
  16.5 1.9 fusion.22
  20.6 7.3 %all-to-all-start = ((bf16[8,4,4,512]{3,2,1,0:T(4,128)(2,1)}), bf16[8,4,4,512]{3,2,1,0:T(4,128)(2,1)S(1)}, u32[]{:S(2)}, u32[]{:S(2)}) async-start(bf16[8,4,4,512]{3,2,1,0:T(4,128)(2,1)} %broadcast_select_fusion.4), calls=%async_computation | async-start | bytes 262144 | tf_op jit(solution)/shard_map/all_to_all | solution.py:75
  28.0 7.4 %all-to-all-done = bf16[8,4,4,512]{3,2,1,0:T(4,128)(2,1)S(1)} async-done(((bf16[8,4,4,512]{3,2,1,0:T(4,128)(2,1)}), bf16[8,4,4,512]{3,2,1,0:T(4,128)(2,1)S(1)}, u32[]{:S(2)}, u32[]{:S(2)}) %all-to-all-start) | async-done | bytes 131104 | tf_op jit(solution)/shard_map/all_to_all | solution.py:75
  36.0 3.3 all-to-all-start.1
  39.7 4.0 gather_fusion.2
  45.0 2.4 copy.101
  50.1 5.1 gather_fusion.1
  55.2 2.4 copy.106
  59.1 1.8 fusion.17
  68.4 4.9 gather_fusion.3
  73.3 3.5 copy.110
  76.8 3.3 multiply_reduce_fusion
  84.0 5.4 fusion.68
  89.3 9.1 %scatter_custom_fusion = f32[1408,512]{1,0:T(8,128)} fusion(s32[1024]{0:T(1024)S(1)} %copy-done.53, f32[1024,1536]{1,0:T(8,128)} %fusion.68, f32[]{:T(128)} %constant.129.clone.1), kind=kCustom, calls=%fused_computation.28 | custom fusion | flops 524288 | bytes 4981248 | tf_op jit(solution)/shard_map/scatter-add | solution.py:162
  98.5 3.1 slice.75
  101.6 2.0 fusion.38
  105.9 3.5 fusion.16
  109.3 267.7 %all-gather.3.cloned.1.call-done = f32[32768,512]{1,0:T(8,128)} async-done(((f32[1024,512]{1,0:T(8,128)}), f32[32768,512]{1,0:T(8,128)}) %all-gather.3.cloned.1.call-update) | async-done | bytes 67108880 | tf_op jit(solution)/shard_map/all_gather | solution.py:62
  377.0 22.1 %reduce_sum.199 = bf16[1024,512]{1,0:T(8,128)(2,1)} reduce(f32[32,1024,512]{2,1,0:T(8,128)} %bitcast.1, f32[]{:T(128)} %constant.129.clone.1), dimensions={0}, to_apply=%region_12.13 | reduce | flops 16252928 | bytes 68157440 | tf_op jit(solution)/shard_map/reduce_sum | solution.py:62
  399.2 2.8 fusion.15
  402.0 2.2 fusion.66
  404.2 3.0 copy.111
  407.2 2.1 multiply_reduce_fusion.1
  415.0 1.9 copy-done.13
  418.5 3.7 gather_fusion.6
  422.2 2.0 multiply_reduce_fusion.5
  427.4 1.8 convolution_add_fusion.2
  429.2 1.9 fusion.70
  431.6 2.3 convolution_add_fusion
  433.9 5.5 scatter_custom_fusion.4
  441.1 3.5 all-to-all-start.2
  445.2 9.2 %all-to-all-done.2 = bf16[8,4,4,512]{3,2,1,0:T(4,128)(2,1)S(1)} async-done(((bf16[8,4,4,512]{3,2,1,0:T(4,128)(2,1)}), bf16[8,4,4,512]{3,2,1,0:T(4,128)(2,1)S(1)}, u32[]{:S(2)}, u32[]{:S(2)}) %all-to-all-start.2) | async-done | bytes 131104 | tf_op jit(solution)/shard_map/all_to_all | solution.py:173
  455.2 3.5 all-to-all-start.3
  460.0 3.1 slice.78
  463.1 3.0 copy.118
  466.1 4.2 add.238
  470.4 2.9 copy.117
  473.2 7.6 %scatter_custom_fusion.1 = f32[256,512]{1,0:T(8,128)S(1)} fusion(f32[256,512]{1,0:T(8,128)S(1)} %fusion.30, s32[1024]{0:T(1024)S(1)} %copy-done.54, f32[1024,1536]{1,0:T(8,128)} %fusion.68), kind=kCustom, calls=%fused_computation.26 | custom fusion | flops 524288 | bytes 2621440 | tf_op jit(solution)/shard_map/scatter-add | solution.py:185
  482.9 3.4 scatter_custom_fusion.2
  487.6 1.7 scatter_fusion
  489.3 39.7 %all-reduce = (f32[512]{0:T(512)S(1)}, f32[512]{0:T(512)S(1)}) all-reduce(f32[512]{0:T(512)S(1)} %add.242, f32[512]{0:T(512)S(1)} %get-tuple-element.78), channel_id=1, replica_groups=mesh['face'=8,'band'=4] {'face','band'}, use_global_device_ids=true, to_apply=%region_27.28 | all-reduce | flops 1024 | bytes 8192 | tf_op jit(solution)/shard_map/psum | solution.py:203
  530.1 2.1 slice_add_fusion
  532.2 99.4 %all-reduce.4.cloned.1.call-done = (f32[1024,512]{1,0:T(8,128)}, f32[1536,512]{1,0:T(8,128)}, f32[512,512]{1,0:T(8,128)}, f32[1024,512]{1,0:T(8,128)}, f32[512,512]{1,0:T(8,128)}) async-done(((f32[1024,512]{1,0:T(8,128)}, f32[1536,512]{1,0:T(8,128)}, f32[512,512]{1,0:T(8,128)}, f32[1024,512]{1,0:T(8,128)}, f32[512,512]{1,0:T(8,128)}), (f32[1024,512]{1,0:T(8,128)}, f32[1536,512]{1,0:T(8,128)}, ...) | async-done | bytes 9437200 | tf_op jit(solution)/shard_map/psum | solution.py:203
  631.7 4.1 fusion.14
  635.8 2.6 add_multiply_fusion
  638.4 2.0 broadcast_multiply_fusion
  642.4 2.0 fusion.7
  (240 shorter events, 51.6 us)
Async XLA Ops:
  7.2 7.0 %copy-start = (bf16[1536,512]{1,0:T(8,128)(2,1)S(1)}, bf16[1536,512]{1,0:T(8,128)(2,1)}, u32[]{:S(2)}) copy-start(bf16[1536,512]{1,0:T(8,128)(2,1)} %param.23) | copy-start | bytes 4718596
  7.2 5.7 copy-start.1
  7.2 369.8 %all-gather.3.cloned.1.call-start = ((), (), s32[]{:S(2)}) async-start(), calls=%async_computation.4 | async-start | bytes 69206016 | tf_op jit(solution)/shard_map/all_gather | solution.py:62
  16.5 1.9 copy-start.52
  18.4 9.5 %copy-start.54 = (s32[1024]{0:T(1024)S(1)}, s32[1024]{0:T(1024)}, u32[]{:S(2)}) copy-start(s32[1024]{0:T(1024)} %param.35) | copy-start | bytes 12292
  18.4 9.5 %copy-start.53 = (s32[1024]{0:T(1024)S(1)}, s32[1024]{0:T(1024)}, u32[]{:S(2)}) copy-start(s32[1024]{0:T(1024)} %param.34) | copy-start | bytes 12292
  20.6 14.7 %all-to-all-start = ((bf16[8,4,4,512]{3,2,1,0:T(4,128)(2,1)}), bf16[8,4,4,512]{3,2,1,0:T(4,128)(2,1)S(1)}, u32[]{:S(2)}, u32[]{:S(2)}) async-start(bf16[8,4,4,512]{3,2,1,0:T(4,128)(2,1)} %broadcast_select_fusion.4), calls=%async_computation | async-start | bytes 262144 | tf_op jit(solution)/shard_map/all_to_all | solution.py:75
  36.0 12.6 %all-to-all-start.1 = ((bf16[8,4,4,512]{3,2,0,1:T(4,128)(2,1)}), bf16[8,4,4,512]{3,2,0,1:T(4,128)(2,1)S(1)}, u32[]{:S(2)}, u32[]{:S(2)}) async-start(bf16[8,4,4,512]{3,2,0,1:T(4,128)(2,1)} %copy.104), calls=%async_computation.1 | async-start | bytes 262144 | tf_op jit(solution)/shard_map/all_to_all | solution.py:74
  39.4 592.3 %all-reduce.4.cloned.1.call-start = ((), (), s32[]{:S(2)}) async-start(), calls=%async_computation.5 | async-start | bytes 18874368 | tf_op jit(solution)/shard_map/psum | solution.py:203
  45.0 2.4 copy-start.32
  55.2 2.4 copy-start.17
  62.6 2.1 copy-start.58
  73.3 3.5 copy-start.15
  76.8 3.4 copy-start.5
  80.2 2.5 copy-start.74
  98.5 3.2 copy-start.46
  98.5 3.2 copy-start.49
  101.6 2.0 copy-start.26
  101.6 2.0 copy-start.68
  103.6 2.3 copy-start.42
  377.0 22.2 %copy-start.8 = (bf16[1024,512]{1,0:T(8,128)(2,1)S(1)}, bf16[1024,512]{1,0:T(8,128)(2,1)}, u32[]{:S(2)}) copy-start(bf16[1024,512]{1,0:T(8,128)(2,1)} %param.20) | copy-start | bytes 3145732
  399.2 2.8 copy-start.59
  402.0 2.2 copy-start.71
  404.2 5.1 copy-start.7
  407.2 2.2 copy-start.2
  410.6 1.9 copy-start.60
  415.0 2.0 copy-start.13
  418.5 3.7 copy-start.11
  418.5 3.7 copy-start.47
  422.2 2.8 copy-start.70
  427.4 3.6 copy-start.31
  427.4 3.6 copy-start.44
  429.1 2.5 copy-start.18
  429.2 2.5 copy-start.29
  439.3 19.4 %copy-start.27 = (bf16[256,512]{1,0:T(8,128)(2,1)S(1)}, bf16[256,512]{1,0:T(8,128)(2,1)}, u32[]{:S(2)}) copy-start(bf16[256,512]{1,0:T(8,128)(2,1)} %param.29) | copy-start | bytes 786436
  441.1 13.4 %all-to-all-start.2 = ((bf16[8,4,4,512]{3,2,1,0:T(4,128)(2,1)}), bf16[8,4,4,512]{3,2,1,0:T(4,128)(2,1)S(1)}, u32[]{:S(2)}, u32[]{:S(2)}) async-start(bf16[8,4,4,512]{3,2,1,0:T(4,128)(2,1)} %convert_element_type.97), calls=%async_computation.2 | async-start | bytes 262144 | tf_op jit(solution)/shard_map/all_to_all | solution.py:173
  455.2 25.7 %all-to-all-start.3 = ((bf16[8,4,4,512]{3,2,0,1:T(4,128)(2,1)}), bf16[8,4,4,512]{3,2,0,1:T(4,128)(2,1)S(1)}, u32[]{:S(2)}, u32[]{:S(2)}) async-start(bf16[8,4,4,512]{3,2,0,1:T(4,128)(2,1)} %copy.113), calls=%async_computation.3 | async-start | bytes 262144 | tf_op jit(solution)/shard_map/all_to_all | solution.py:172
  480.9 5.4 copy-start.21
  480.9 5.4 copy-start.55
  489.3 146.4 %copy-start.6 = (f32[256,512]{1,0:T(8,128)}, f32[256,512]{1,0:T(8,128)S(1)}, u32[]{:S(2)}) copy-start(f32[256,512]{1,0:T(8,128)S(1)} %scatter_fusion) | copy-start | bytes 1572868
  631.7 4.1 copy-start.9
  631.7 4.1 copy-start.22
  631.7 4.1 copy-start.57
  631.7 4.1 copy-start.66
  635.8 2.6 copy-start.19
  638.4 3.3 copy-start.14
  638.4 4.0 copy-start.20
  642.4 2.0 copy-start.35
  (34 other events, 45.7 us)
Sparse Core Ops, SparseCore 0:
  18.6 358.3 all-gather.2
  439.5 192.1 all-reduce.3
